TPU v7x, 256 devices: a whole 4x4x8 slice. The times are simulated.
256 devices in a mesh: layer: 4 (over x_lo, core), feat: 64 (over x_hi, z, y).
Axes of the slice: x: 4 (x_hi: 2, x_lo: 2; x = x_hi * 2 + x_lo), y: 4, z: 8, core: 2. Of those that a mesh axis runs over, the one named last changes fastest.
Arguments:
- sources: bfloat16 [4, 512, 4096], P('layer', 'feat'), may hold values from -6 to 6
- targets: bfloat16 [4, 512, 4096], P('layer', 'feat'), may hold values from -6 to 6
- enc_weight: bfloat16 [4, 8192, 4096], P('layer', 'feat'), may hold values from -0.09375 to 0.09375
- dec_weight: bfloat16 [4, 4, 8192, 4096], P('layer', None, 'feat'), may hold values from -0.0625 to 0.0625
- active: int32 [4, 8192, 512], P('layer', 'feat'), may hold values 0 or 1
Outputs:
- errors: float32 [4, 512, 4096], P('layer', 'feat')
- grad_dec: bfloat16 [4, 4, 8192, 4096], P('layer', None, 'feat')
- grad_enc: bfloat16 [4, 8192, 4096], P('layer', 'feat')
All inputs are finite; a program needn't handle non-finite values. No bound on the sum of `active` on one device may be relied on, other than what follows from the above.
Results may differ from a plain program's by a relative error of at most 0.0061.
Values may be sent and summed in bfloat16 or wider, within the bound.
No kernel may reach another device: no remote copies, remote signals or barrier semaphores. Data moves between devices by JAX's collectives and lax.ppermute only.
A program may use at most 64 MiB of HBM per device.

v0:
```python
import math
import jax
import jax.numpy as jnp
from jax import lax
from jax.sharding import PartitionSpec as P

TOKENS = 512


def on_device(sources, targets, enc_weight, dec_weight, active):
    per_group = sources.shape[0]
    layer_count = dec_weight.shape[1]
    group_index = lax.axis_index("layer")
    source_full = lax.all_gather(sources, "feat", axis=1, tiled=True)
    pre_acts = jnp.einsum(
        "sfd,std->sft", enc_weight, source_full, preferred_element_type=jnp.float32
    )
    features = (active.astype(jnp.float32) * pre_acts).astype(jnp.bfloat16)
    all_features = lax.all_gather(features, "layer", axis=0, tiled=True)
    target_pos = group_index * per_group + jnp.arange(per_group, dtype=jnp.int32)
    source_pos = jnp.arange(layer_count, dtype=jnp.int32)
    causal = source_pos[None, :] <= target_pos[:, None]
    masked = all_features[None] * causal[:, :, None, None].astype(jnp.bfloat16)
    recon_terms = jnp.einsum(
        "slft,slfd->std", masked, dec_weight, preferred_element_type=jnp.float32
    )
    scale = 1.0 / math.sqrt(TOKENS)
    recon_sum = lax.psum_scatter(recon_terms, "feat", scatter_dimension=1, tiled=True)
    errors = recon_sum - targets.astype(jnp.float32)
    scaled_error = (errors * scale).astype(jnp.bfloat16)
    scaled_full = lax.all_gather(scaled_error, "feat", axis=1, tiled=True)
    grad_dec = jnp.einsum(
        "slft,std->slfd", masked, scaled_full, preferred_element_type=jnp.float32
    ).astype(jnp.bfloat16)
    partial_grad = jnp.einsum(
        "slfd,std->slft", dec_weight, scaled_full, preferred_element_type=jnp.float32
    )
    partial_grad = jnp.sum(partial_grad * causal[:, :, None, None].astype(jnp.float32), axis=0)
    feature_grad = lax.psum_scatter(partial_grad, "layer", scatter_dimension=0, tiled=True)
    pre_grad = (active.astype(jnp.float32) * feature_grad).astype(jnp.bfloat16)
    grad_enc = jnp.einsum(
        "sft,std->sfd", pre_grad, source_full, preferred_element_type=jnp.float32
    ).astype(jnp.bfloat16)
    return (errors, grad_dec, grad_enc)


def solution(mesh):
    in_specs = (
        P("layer", "feat", None),
        P("layer", "feat", None),
        P("layer", "feat", None),
        P("layer", None, "feat", None),
        P("layer", "feat", None),
    )
    out_specs = (P("layer", "feat", None), P("layer", None, "feat", None), P("layer", "feat", None))
    return jax.shard_map(
        on_device, mesh=mesh, in_specs=in_specs, out_specs=out_specs, check_vma=False
    )
```

profile of v0, /device:TPU:1, one launch (start us, length us, event | category | flops | bytes accessed | tf_op | source)
XLA Modules:
  0.0 701.5 jit_solution(4639413504859999546)
XLA Ops:
  7.2 0.0 copy-start
  7.2 0.0 all-gather.3.cloned.1.call-start
  7.2 0.7 all-gather.3.cloned.1.call-update
  7.9 0.0 reduce-scatter.3.cloned.1.call-start
  8.0 131.2 %all-gather.3.cloned.1.call-done = bf16[1,512,4096]{2,1,0:T(8,128)(2,1)} async-done(((bf16[1,8,4096]{2,1,0:T(8,128)(2,1)}), bf16[1,512,4096]{2,1,0:T(8,128)(2,1)}) %all-gather.3.cloned.1.call-update) | async-done | bytes 4194320 | tf_op jit(solution)/shard_map/all_gather | solution.py:14
  139.2 0.0 copy-done
  139.2 0.0 copy-start.1
  139.2 3.9 fusion.26
  143.1 10.6 %all_gather.10 = bf16[4,128,512]{2,1,0:T(8,128)(2,1)S(1)} all-gather(bf16[1,128,512]{2,1,0:T(8,128)(2,1)S(1)} %fusion.26), channel_id=1, replica_groups=mesh['layer'=4,'feat'=64] {'layer'}, dimensions={0}, use_global_device_ids=true | all-gather | bytes 655360 | tf_op jit(solution)/shard_map/all_gather | solution.py:19
  153.7 0.0 copy-done.1
  153.7 5.7 convolution_bitcast_fusion
  159.4 0.0 copy-start.3
  159.4 0.0 reduce-scatter.3.cloned.1.call-update
  159.5 0.0 all-gather.5.cloned.1.call-start
  159.5 334.9 %reduce-scatter.3.cloned.1.call-done = f32[1,8,4096]{2,1,0:T(8,128)} async-done(((f32[1,512,4096]{2,1,0:T(8,128)}), f32[1,8,4096]{2,1,0:T(8,128)}) %reduce-scatter.3.cloned.1.call-update) | async-done | bytes 131088 | tf_op jit(solution)/shard_map/reduce_scatter | solution.py:28
  494.4 0.0 copy-done.3
  494.4 1.6 multiply_convert_fusion.1
  496.0 0.0 all-gather.5.cloned.1.call-update
  496.0 0.0 reduce-scatter.5.cloned.1.call-start
  496.1 164.2 %all-gather.5.cloned.1.call-done = bf16[1,512,4096]{2,1,0:T(8,128)(2,1)} async-done(((bf16[1,8,4096]{2,1,0:T(8,128)(2,1)}), bf16[1,512,4096]{2,1,0:T(8,128)(2,1)}) %all-gather.5.cloned.1.call-update) | async-done | bytes 4194320 | tf_op jit(solution)/shard_map/all_gather | solution.py:31
  660.3 6.8 fusion.15
  667.1 0.0 reduce-scatter.5.cloned.1.call-update
  667.1 0.0 copy-start.2
  667.1 6.6 fusion
  673.7 17.2 %reduce-scatter.5.cloned.1.call-done = f32[1,128,512]{2,1,0:T(8,128)} async-done(((f32[4,128,512]{2,1,0:T(8,128)}), f32[1,128,512]{2,1,0:T(8,128)}) %reduce-scatter.5.cloned.1.call-update) | async-done | bytes 262160 | tf_op jit(solution)/shard_map/reduce_scatter | solution.py:39
  691.0 0.0 copy-done.2
  691.0 4.0 fusion.1
  (2 shorter events, 0.0 us)
Async XLA Ops:
  7.2 132.1 %copy-start = (bf16[1,128,4096]{2,1,0:T(8,128)(2,1)S(1)}, bf16[1,128,4096]{2,1,0:T(8,128)(2,1)}, u32[]{:S(2)}) copy-start(bf16[1,128,4096]{2,1,0:T(8,128)(2,1)} %param.7) | copy-start | bytes 3145732
  7.2 132.0 %all-gather.3.cloned.1.call-start = ((), (), s32[]{:S(2)}) async-start(), calls=%async_computation.2 | async-start | bytes 4259840 | tf_op jit(solution)/shard_map/all_gather | solution.py:14
  7.9 486.5 %reduce-scatter.3.cloned.1.call-start = ((), (), s32[]{:S(2)}) async-start(), calls=%async_computation.3 | async-start | bytes 8519680 | tf_op jit(solution)/shard_map/reduce_scatter | solution.py:28
  139.2 14.5 %copy-start.1 = (bf16[1,4,128,4096]{3,2,1,0:T(8,128)(2,1)S(1)}, bf16[1,4,128,4096]{3,2,1,0:T(8,128)(2,1)}, u32[]{:S(2)}) copy-start(bf16[1,4,128,4096]{3,2,1,0:T(8,128)(2,1)} %param.8) | copy-start | bytes 12582916
  159.4 335.0 %copy-start.3 = (bf16[1,8,4096]{2,1,0:T(8,128)(2,1)S(1)}, bf16[1,8,4096]{2,1,0:T(8,128)(2,1)}, u32[]{:S(2)}) copy-start(bf16[1,8,4096]{2,1,0:T(8,128)(2,1)} %param.6) | copy-start | bytes 196612
  159.5 500.8 %all-gather.5.cloned.1.call-start = ((), (), s32[]{:S(2)}) async-start(), calls=%async_computation.4 | async-start | bytes 4259840 | tf_op jit(solution)/shard_map/all_gather | solution.py:31
  496.0 194.9 %reduce-scatter.5.cloned.1.call-start = ((), (), s32[]{:S(2)}) async-start(), calls=%async_computation.5 | async-start | bytes 1310720 | tf_op jit(solution)/shard_map/reduce_scatter | solution.py:39
  667.1 23.9 %copy-start.2 = (s32[1,128,512]{2,1,0:T(8,128)S(1)}, s32[1,128,512]{2,1,0:T(8,128)}, u32[]{:S(2)}) copy-start(s32[1,128,512]{2,1,0:T(8,128)} %param.9) | copy-start | bytes 786436
Sparse Core Ops, SparseCore 0:
  11.5 127.6 all-gather.2
  159.6 334.7 reduce-scatter.2
  498.5 161.7 all-gather.4
  667.2 23.6 reduce-scatter.4
where the time goes:
time: 702 us; the launch traced here: 701 us
  waiting for transfers between devices  648 us (92%)
  matrix products  27 us (4%)
  between operations  13.8 us (2%)
  blocking collectives  10.6 us (2%)
    reduce_scatter x1, waiting for transfers between devices, on_device(): lax.psum_scatter(recon_terms, 'feat', scatter_dimension=1, tiled=True)  335 us
    all_gather x1, waiting for transfers between devices, on_device(): scaled_full = lax.all_gather(scaled_error, 'feat', axis=1, tiled=True)  164 us
    all_gather x1, waiting for transfers between devices, on_device(): source_full = lax.all_gather(sources, 'feat', axis=1, tiled=True)  131 us
    reduce_scatter x1, waiting for transfers between devices, on_device(): lax.psum_scatter(partial_grad, 'layer', scatter_dimension=0, tiled=True)  17.2 us
  transfers between devices with their start and end apart: 4, of which 4 were waited for; matrix products, arithmetic and copies ran while one was open for 1% of the time, Pallas kernels for 0%

commit v1 on v0

--- a/solution.py
+++ b/solution.py
@@ -28,7 +28,9 @@
     recon_sum = lax.psum_scatter(recon_terms, "feat", scatter_dimension=1, tiled=True)
     errors = recon_sum - targets.astype(jnp.float32)
     scaled_error = (errors * scale).astype(jnp.bfloat16)
-    scaled_full = lax.all_gather(scaled_error, "feat", axis=1, tiled=True)
+    scaled_full = jnp.concatenate(
+        lax.all_to_all(jnp.stack([scaled_error] * lax.axis_size("feat")), "feat", 0, 0), axis=1
+    )
     grad_dec = jnp.einsum(
         "slft,std->slfd", masked, scaled_full, preferred_element_type=jnp.float32
     ).astype(jnp.bfloat16)

time: 702 us -> 648 us (0.923)
  waiting for transfers between devices: 648 us -> 587 us
    all_gather x1 -> x0, waiting for transfers between devices: 164 us -> none  [on_device(): scaled_full = lax.all_gather(scaled_error, 'feat', axis=1, tiled=True)]
    reduce_scatter x1, waiting for transfers between devices: 17.2 us -> 69 us  [on_device(): lax.psum_scatter(partial_grad, 'layer', scatter_dimension=0, tiled=True)]
    all_to_all x0 -> x1, waiting for transfers between devices: none -> 51 us  [on_device(): lax.all_to_all(jnp.stack([scaled_error] * lax.axis_size('feat')), 'feat',...]
where the time goes in v1:
time: 648 us
  waiting for transfers between devices  587 us (91%)
  matrix products  27 us (4%)
  between operations  13.8 us (2%)
  blocking collectives  10.6 us (2%)
    reduce_scatter x1, waiting for transfers between devices, on_device(): lax.psum_scatter(recon_terms, 'feat', scatter_dimension=1, tiled=True)  335 us
    all_gather x1, waiting for transfers between devices, on_device(): source_full = lax.all_gather(sources, 'feat', axis=1, tiled=True)  131 us
    reduce_scatter x1, waiting for transfers between devices, on_device(): lax.psum_scatter(partial_grad, 'layer', scatter_dimension=0, tiled=True)  69 us
    all_to_all x1, waiting for transfers between devices, on_device(): lax.all_to_all(jnp.stack([scaled_error] * lax.axis_size('feat')), 'feat',...  51 us
  transfers between devices with their start and end apart: 4, of which 4 were waited for; matrix products, arithmetic and copies ran while one was open for 1% of the time, Pallas kernels for 0%

profile of v1, /device:TPU:1, one launch (start us, length us, event | category | flops | bytes accessed | tf_op | source)
XLA Modules:
  0.0 648.1 jit_solution(1283506643641131814)
XLA Ops:
  7.2 0.0 copy-start
  7.2 0.0 all-gather.2.cloned.1.call-start
  7.2 0.7 all-gather.2.cloned.1.call-update
  7.9 0.0 reduce-scatter.3.cloned.1.call-start
  8.0 131.2 %all-gather.2.cloned.1.call-done = bf16[1,512,4096]{2,1,0:T(8,128)(2,1)} async-done(((bf16[1,8,4096]{2,1,0:T(8,128)(2,1)}), bf16[1,512,4096]{2,1,0:T(8,128)(2,1)}) %all-gather.2.cloned.1.call-update) | async-done | bytes 4194320 | tf_op jit(solution)/shard_map/all_gather | solution.py:14
  139.2 0.0 copy-done
  139.2 0.0 copy-start.1
  139.2 3.9 fusion.26
  143.1 10.6 %all_gather.7 = bf16[4,128,512]{2,1,0:T(8,128)(2,1)S(1)} all-gather(bf16[1,128,512]{2,1,0:T(8,128)(2,1)S(1)} %fusion.26), channel_id=1, replica_groups=mesh['layer'=4,'feat'=64] {'layer'}, dimensions={0}, use_global_device_ids=true | all-gather | bytes 655360 | tf_op jit(solution)/shard_map/all_gather | solution.py:19
  153.7 0.0 copy-done.1
  153.7 5.7 convolution_bitcast_fusion
  159.4 0.0 copy-start.3
  159.4 0.0 reduce-scatter.3.cloned.1.call-update
  159.5 334.9 %reduce-scatter.3.cloned.1.call-done = f32[1,8,4096]{2,1,0:T(8,128)} async-done(((f32[1,512,4096]{2,1,0:T(8,128)}), f32[1,8,4096]{2,1,0:T(8,128)}) %reduce-scatter.3.cloned.1.call-update) | async-done | bytes 131088 | tf_op jit(solution)/shard_map/reduce_scatter | solution.py:28
  494.4 0.0 copy-done.3
  494.4 1.6 fusion.36
  496.0 2.5 stack.2
  498.5 5.7 all-to-all-start
  504.2 0.0 reduce-scatter.5.cloned.1.call-start
  504.2 51.0 %all-to-all-done = bf16[64,1,8,4096]{3,2,1,0:T(8,128)(2,1)} async-done(((bf16[64,1,8,4096]{3,2,1,0:T(8,128)(2,1)}), bf16[64,1,8,4096]{3,2,1,0:T(8,128)(2,1)}, u32[]{:S(2)}, u32[]{:S(2)}) %all-to-all-start) | async-done | bytes 4194336 | tf_op jit(solution)/shard_map/all_to_all | solution.py:32
  555.2 6.8 %fusion.15 = f32[4,128,512]{2,1,0:T(8,128)} fusion(bf16[1,4,128,4096]{3,2,1,0:T(8,128)(2,1)} %param.8, bf16[64,1,8,4096]{3,2,1,0:T(8,128)(2,1)} %all-to-all-done, f32[4]{0:T(128)S(1)} %compare_convert_fusion), kind=kOutput, calls=%fused_computation.14 | convolution fusion | flops 2147745792 | bytes 9437200 | tf_op jit(solution)/shard_map/slfd,std->slft/dot_general | solution.py:37
  562.0 0.0 reduce-scatter.5.cloned.1.call-update
  562.0 0.0 copy-start.2
  562.1 6.6 %fusion = bf16[1,4,128,4096]{3,2,1,0:T(8,128)(2,1)} fusion(bf16[64,1,8,4096]{3,2,1,0:T(8,128)(2,1)} %all-to-all-done, bf16[4,128,512]{2,1,0:T(8,128)(2,1)S(1)} %all_gather.7, bf16[4]{0:T(256)(128)(2,1)S(1)} %compare_convert_fusion.1), kind=kOutput, calls=%fused_computation.2 | convolution fusion | flops 2149842944 | bytes 8912904 | tf_op jit(solution)/shard_map/slft,std->slfd/dot_general | solution.py:34
  568.7 69.0 %reduce-scatter.5.cloned.1.call-done = f32[1,128,512]{2,1,0:T(8,128)} async-done(((f32[4,128,512]{2,1,0:T(8,128)}), f32[1,128,512]{2,1,0:T(8,128)}) %reduce-scatter.5.cloned.1.call-update) | async-done | bytes 262160 | tf_op jit(solution)/shard_map/reduce_scatter | solution.py:41
  637.6 0.0 copy-done.2
  637.6 4.0 fusion.1
  (2 shorter events, 0.0 us)
Async XLA Ops:
  7.2 132.1 %copy-start = (bf16[1,128,4096]{2,1,0:T(8,128)(2,1)S(1)}, bf16[1,128,4096]{2,1,0:T(8,128)(2,1)}, u32[]{:S(2)}) copy-start(bf16[1,128,4096]{2,1,0:T(8,128)(2,1)} %param.7) | copy-start | bytes 3145732
  7.2 132.0 %all-gather.2.cloned.1.call-start = ((), (), s32[]{:S(2)}) async-start(), calls=%async_computation.3 | async-start | bytes 4259840 | tf_op jit(solution)/shard_map/all_gather | solution.py:14
  7.9 486.5 %reduce-scatter.3.cloned.1.call-start = ((), (), s32[]{:S(2)}) async-start(), calls=%async_computation.4 | async-start | bytes 8519680 | tf_op jit(solution)/shard_map/reduce_scatter | solution.py:28
  139.2 14.5 %copy-start.1 = (bf16[1,4,128,4096]{3,2,1,0:T(8,128)(2,1)S(1)}, bf16[1,4,128,4096]{3,2,1,0:T(8,128)(2,1)}, u32[]{:S(2)}) copy-start(bf16[1,4,128,4096]{3,2,1,0:T(8,128)(2,1)} %param.8) | copy-start | bytes 12582916
  159.4 335.0 %copy-start.3 = (bf16[1,8,4096]{2,1,0:T(8,128)(2,1)S(1)}, bf16[1,8,4096]{2,1,0:T(8,128)(2,1)}, u32[]{:S(2)}) copy-start(bf16[1,8,4096]{2,1,0:T(8,128)(2,1)} %param.6) | copy-start | bytes 196612
  498.5 56.7 %all-to-all-start = ((bf16[64,1,8,4096]{3,2,1,0:T(8,128)(2,1)}), bf16[64,1,8,4096]{3,2,1,0:T(8,128)(2,1)}, u32[]{:S(2)}, u32[]{:S(2)}) async-start(bf16[64,1,8,4096]{3,2,1,0:T(8,128)(2,1)} %stack.2), calls=%async_computation.1 | async-start | bytes 8388608 | tf_op jit(solution)/shard_map/all_to_all | solution.py:32
  504.2 133.5 %reduce-scatter.5.cloned.1.call-start = ((), (), s32[]{:S(2)}) async-start(), calls=%async_computation.5 | async-start | bytes 1310720 | tf_op jit(solution)/shard_map/reduce_scatter | solution.py:41
  562.0 75.6 %copy-start.2 = (s32[1,128,512]{2,1,0:T(8,128)S(1)}, s32[1,128,512]{2,1,0:T(8,128)}, u32[]{:S(2)}) copy-start(s32[1,128,512]{2,1,0:T(8,128)} %param.9) | copy-start | bytes 786436
Sparse Core Ops, SparseCore 0:
  11.5 127.6 all-gather.1
  159.6 334.7 reduce-scatter.2
  562.2 75.4 reduce-scatter.4
